TPU v7x, 512 devices: a whole 4x4x16 slice. The times are simulated.
512 devices in a mesh: seq: 64 (over x_hi, z, core), head: 8 (over x_lo, y).
Axes of the slice: x: 4 (x_hi: 2, x_lo: 2; x = x_hi * 2 + x_lo), y: 4, z: 16, core: 2. Of those that a mesh axis runs over, the one named last changes fastest.
Arguments:
- queries: bfloat16 [24576, 8192], P(('seq', 'head')), may hold values from -26 to 26
- keys: bfloat16 [24576, 1024], P(('seq', 'head')), may hold values from -6 to 6
- values: bfloat16 [24576, 1024], P(('seq', 'head')), may hold values from -6 to 6
- block_list: int32 [8, 192, 32], replicated, may hold values from 0 to 191, as said below
- block_count: int32 [8, 192], replicated, may hold values from 1 to 32
Outputs:
- attended: bfloat16 [24576, 8192], P(('seq', 'head'))
Inputs may be any that keep to these rules, and one draw needn't show every extreme that they name: `block_list`: for each key-value head and query block b, the used entries are distinct key blocks, none after b, and unused entries are 0. For each key-value head, the query blocks of one sequence shard (3 blocks) together list at most one block of each other shard, from at most 29 other shards.
All inputs are finite; a program needn't handle non-finite values.
Results may differ from a plain program's by a relative error of at most 0.0045.
Values may be sent and summed in bfloat16 or wider, within the bound.
A program may use at most 64 MiB of HBM per device.

v0:
```python
import math

import jax
import jax.numpy as jnp
from jax import lax
from jax.sharding import PartitionSpec as P

HEADS = 64
KV_HEADS = 8
HEAD_DIM = 128
BLOCK = 128
STEP = 8
TOK_DEV = 384


def attend_block(
    block_q, kv_table, entries, listed_count, query_position, my_shard, shards, per_shard
):
    inverse_root = 1.0 / math.sqrt(HEAD_DIM)
    per_kv = block_q.shape[1]
    offsets = jnp.arange(BLOCK, dtype=jnp.int32)

    def step_once(step_index, carried):
        running, denominator, accumulated = carried
        selected = lax.dynamic_slice_in_dim(entries, step_index * STEP, STEP)
        owners = selected // per_shard
        location = jnp.where(owners == my_shard, shards + selected % per_shard, owners)
        fetched_rows = jnp.take(kv_table, location, axis=0).reshape(STEP * BLOCK, 2 * HEAD_DIM)
        key_rows = fetched_rows[:, :HEAD_DIM]
        value_rows = fetched_rows[:, HEAD_DIM:]
        key_position = (selected[:, None] * BLOCK + offsets[None, :]).reshape(-1)
        usable = jnp.repeat(
            step_index * STEP + jnp.arange(STEP, dtype=jnp.int32) < listed_count, BLOCK
        )
        allowed = usable[None, :] & (key_position[None, :] <= query_position[:, None])
        scores = (
            jnp.einsum("qhd,kd->hqk", block_q, key_rows, preferred_element_type=jnp.float32)
            * inverse_root
        )
        scores = jnp.where(allowed[None, :, :], scores, jnp.float32(-1e30))
        newest = jnp.maximum(running, jnp.max(scores, axis=-1))
        rescale = jnp.exp(running - newest)
        prob = jnp.exp(scores - newest[..., None])
        denominator = denominator * rescale + jnp.sum(prob, axis=-1)
        weights = prob.astype(jnp.bfloat16)
        accumulated = accumulated * rescale[..., None] + jnp.einsum(
            "hqk,kd->hqd", weights, value_rows, preferred_element_type=jnp.float32
        )
        return (newest, denominator, accumulated)

    initial = (
        jnp.full((per_kv, BLOCK), -1e30, jnp.float32),
        jnp.zeros((per_kv, BLOCK), jnp.float32),
        jnp.zeros((per_kv, BLOCK, HEAD_DIM), jnp.float32),
    )
    running, denominator, accumulated = lax.fori_loop(
        0, (listed_count + STEP - 1) // STEP, step_once, initial
    )
    result = accumulated / denominator[..., None]
    return result.transpose(1, 0, 2).reshape(BLOCK, per_kv * HEAD_DIM).astype(jnp.bfloat16)


def per_device(queries, keys, values, block_list, block_count):
    query_local, key_local, value_local = (
        lax.all_to_all(queries, "head", split_axis=1, concat_axis=0, tiled=True),
        lax.all_to_all(keys, "head", split_axis=1, concat_axis=0, tiled=True),
        lax.all_to_all(values, "head", split_axis=1, concat_axis=0, tiled=True),
    )
    shards = lax.axis_size("seq")
    my_shard = lax.axis_index("seq")
    head_group = lax.axis_index("head")
    kv_dev = key_local.shape[1] // HEAD_DIM
    per_shard = TOK_DEV // BLOCK
    per_kv = HEADS // KV_HEADS
    list_width = block_list.shape[2]
    listed = lax.dynamic_slice_in_dim(block_list, head_group * kv_dev, kv_dev, 0)
    counted = lax.dynamic_slice_in_dim(block_count, head_group * kv_dev, kv_dev, 0)
    usable = jnp.arange(list_width, dtype=jnp.int32)[None, None, :] < counted[:, :, None]
    kv_pairs = jnp.concatenate(
        [
            key_local.reshape(TOK_DEV, kv_dev, HEAD_DIM),
            value_local.reshape(TOK_DEV, kv_dev, HEAD_DIM),
        ],
        axis=2,
    )
    kv_pairs = kv_pairs.reshape(per_shard, BLOCK, kv_dev, 2 * HEAD_DIM)
    readers = jnp.arange(shards, dtype=jnp.int32)
    block_ids = jnp.arange(per_shard, dtype=jnp.int32)
    own_entries = lax.dynamic_slice_in_dim(listed, my_shard * per_shard, per_shard, 1)
    own_entries = own_entries.reshape(kv_dev, per_shard * list_width)
    own_usable = lax.dynamic_slice_in_dim(usable, my_shard * per_shard, per_shard, 1)
    own_usable = own_usable.reshape(kv_dev, per_shard * list_width)
    needed = own_usable[:, :, None] & (
        (own_entries // per_shard)[:, :, None] == readers[None, None, :]
    )
    needed = needed & (readers[None, None, :] != my_shard)
    wanted = jnp.max(jnp.where(needed, (own_entries % per_shard)[:, :, None], -1), axis=1)
    onehot = (wanted[:, :, None] == block_ids[None, None, :]).astype(jnp.bfloat16)
    fetched = jnp.einsum(
        "jnb,nbrjc->nrjc",
        onehot,
        lax.all_gather(kv_pairs[None], "seq", axis=0, tiled=True),
        preferred_element_type=jnp.float32,
    ).astype(jnp.bfloat16)
    kv_table = jnp.concatenate([fetched, kv_pairs], axis=0)
    offsets = jnp.arange(BLOCK, dtype=jnp.int32)
    row_parts = []
    for local_block in range(per_shard):
        query_block = my_shard * per_shard + local_block
        query_position = query_block * BLOCK + offsets
        entries = lax.dynamic_index_in_dim(listed[0], query_block, 0, False)
        listed_count = lax.dynamic_index_in_dim(counted[0], query_block, 0, False)
        block_q = query_local[
            local_block * BLOCK : (local_block + 1) * BLOCK, 0 : per_kv * HEAD_DIM
        ]
        block_q = block_q.reshape(BLOCK, per_kv, HEAD_DIM)
        columns = attend_block(
            block_q,
            kv_table[:, :, 0],
            entries,
            listed_count,
            query_position,
            my_shard,
            shards,
            per_shard,
        )
        row_parts.append(columns)
    attended_local = jnp.concatenate(row_parts, axis=0)
    return lax.all_to_all(attended_local, "head", split_axis=0, concat_axis=1, tiled=True)


def solution(mesh):
    placed = (
        P(("seq", "head"), None),
        P(("seq", "head"), None),
        P(("seq", "head"), None),
        P(),
        P(),
    )
    return jax.shard_map(
        per_device, mesh=mesh, in_specs=placed, out_specs=P(("seq", "head"), None), check_vma=False
    )
```

profile of v0, /device:TPU:4, one launch (start us, length us, event | category | flops | bytes accessed | tf_op | source)
XLA Modules:
  0.0 345.6 jit_solution(10866311652212428212)
XLA Ops:
  6.5 0.9 copy-done
  8.1 5.1 %all-to-all-start = ((bf16[48,8,128]{2,0,1:T(8,128)(2,1)}), bf16[48,8,128]{2,0,1:T(8,128)(2,1)S(1)}, u32[]{:S(2)}, u32[]{:S(2)}) async-start(bf16[48,8,128]{2,0,1:T(8,128)(2,1)} %copy_bitcast_fusion.2), calls=%async_computation | async-start | bytes 196608 | tf_op jit(solution)/shard_map/all_to_all | solution.py:66
  13.2 0.9 copy_bitcast_fusion.1
  14.2 5.5 %all-to-all-done = bf16[48,8,128]{2,0,1:T(8,128)(2,1)S(1)} async-done(((bf16[48,8,128]{2,0,1:T(8,128)(2,1)}), bf16[48,8,128]{2,0,1:T(8,128)(2,1)S(1)}, u32[]{:S(2)}, u32[]{:S(2)}) %all-to-all-start) | async-done | bytes 98336 | tf_op jit(solution)/shard_map/all_to_all | solution.py:66
  19.6 8.9 %all_to_all.70 = bf16[48,8,128]{2,0,1:T(8,128)(2,1)S(1)} all-to-all(bf16[48,8,128]{2,0,1:T(8,128)(2,1)S(1)} %copy_bitcast_fusion.1), channel_id=1, replica_groups=mesh['seq'=64,'head'=8] {'head'}, dimensions={1} | all-to-all | bytes 196608 | tf_op jit(solution)/shard_map/all_to_all | solution.py:67
  29.3 2.1 copy.132
  31.4 3.5 %all-to-all-start.2 = ((bf16[48,8,1024]{2,0,1:T(8,128)(2,1)}), bf16[48,8,1024]{2,0,1:T(8,128)(2,1)S(1)}, u32[]{:S(2)}, u32[]{:S(2)}) async-start(bf16[48,8,1024]{2,0,1:T(8,128)(2,1)} %bitcast.134), calls=%async_computation.2 | async-start | bytes 1572864 | tf_op jit(solution)/shard_map/all_to_all | solution.py:65
  34.9 0.8 constant_dynamic-slice_fusion
  36.7 1.4 fusion.62
  40.4 1.1 dynamic-slice_reduce_fusion.2
  41.8 3.0 all-to-all-done.2
  46.0 163.5 %all-gather.2.cloned.1.call-done = bf16[64,3,128,1,256]{4,2,3,1,0:T(8,128)(2,1)} async-done(((bf16[1,3,128,1,256]{4,2,3,1,0:T(8,128)(2,1)}), bf16[64,3,128,1,256]{4,2,3,1,0:T(8,128)(2,1)}) %all-gather.2.cloned.1.call-update) | async-done | bytes 12582928 | tf_op jit(solution)/shard_map/all_gather | solution.py:102
  209.5 17.6 %fusion.54 = bf16[64,1,128,256]{3,1,2,0:T(2,128)(2,1)S(1)} fusion(bf16[64,3,128,256]{3,2,1,0:T(8,128)(2,1)} %bitcast.211, pred[64,3,1,1]{1,0,2,3:T(32,128)(4,1)S(1)} %fusion.60), kind=kOutput, calls=%fused_computation.99 | convolution fusion | flops 12582912 | bytes 16777408 | tf_op jit(solution)/shard_map/jnb,nbrjc->nrjc/dot_general | solution.py:99
  227.1 1.2 copy.131
  228.3 2.2 maximum_bitcast_fusion
  230.6 14.4 %while.51 = (s32[]{:T(128)}, f32[8,128]{1,0:T(8,128)S(1)}, f32[8,128]{1,0:T(8,128)S(1)}, f32[8,128,128]{2,1,0:T(8,128)S(1)}, s32[]{:T(128)}, /*index=5*/s32[]{:T...) while((s32[]{:T(128)}, f32[8,128]{1,0:T(8,128)S(1)}, ...), condition=%wide.region_4.6_spmd.clone, body=%wide.region_1.5_spmd.clone.sunk | while | flops 549196096 | bytes 17120724 | solution.py:56
  231.3 2.8 gather_fusion
  234.8 0.8 fusion.89
  235.6 0.9 fusion.90
  236.5 1.3 fusion.91
  238.5 2.8 gather_fusion
  242.1 0.8 fusion.89
  242.9 0.9 fusion.90
  243.8 1.3 fusion.91
  245.3 14.7 %while.52 = (s32[]{:T(128)}, f32[8,128]{1,0:T(8,128)S(1)}, f32[8,128]{1,0:T(8,128)S(1)}, f32[8,128,128]{2,1,0:T(8,128)S(1)}, s32[]{:T(128)}, /*index=5*/s32[]{:T...) while((s32[]{:T(128)}, f32[8,128]{1,0:T(8,128)S(1)}, ...), condition=%wide.region_8.10_spmd.clone, body=%wide.region_5.9_spmd.clone.sunk | while | flops 549196096 | bytes 17120724 | solution.py:56
  245.5 0.7 compare_and_fusion.14
  246.3 2.8 gather_fusion.1
  249.8 0.8 fusion.95
  250.6 0.9 fusion.96
  251.5 1.3 fusion.97
  252.8 0.7 compare_and_fusion.14
  253.5 2.8 gather_fusion.1
  257.1 0.8 fusion.95
  257.8 0.9 fusion.96
  258.7 1.3 fusion.97
  260.3 14.5 %while.53 = (s32[]{:T(128)}, f32[8,128]{1,0:T(8,128)S(1)}, f32[8,128]{1,0:T(8,128)S(1)}, f32[8,128,128]{2,1,0:T(8,128)S(1)}, s32[]{:T(128)}, /*index=5*/s32[]{:T...) while((s32[]{:T(128)}, f32[8,128]{1,0:T(8,128)S(1)}, ...), condition=%wide.region_12.14_spmd.clone, body=%wide.region_9.13_spmd.clone.sunk | while | flops 549196096 | bytes 17120724 | solution.py:56
  260.3 0.7 compare_and_fusion.16
  261.1 2.8 gather_fusion.2
  264.6 0.8 fusion.101
  265.4 0.9 fusion.102
  266.3 1.3 fusion.103
  267.6 0.7 compare_and_fusion.16
  268.4 2.8 gather_fusion.2
  271.9 0.8 fusion.101
  272.7 0.9 fusion.102
  273.6 1.3 fusion.103
  275.7 62.2 %all_to_all.71 = bf16[8,48,1024]{2,1,0:T(8,128)(2,1)S(1)} all-to-all(bf16[8,48,1024]{2,1,0:T(8,128)(2,1)S(1)} %bitcast.197), channel_id=1, replica_groups=mesh['seq'=64,'head'=8] {'head'}, dimensions={0} | all-to-all | bytes 1572864 | tf_op jit(solution)/shard_map/all_to_all | solution.py:129
  337.8 0.9 copy.120
  (105 shorter events, 11.0 us)
Async XLA Ops:
  6.5 0.9 copy-start
  8.1 11.5 %all-to-all-start = ((bf16[48,8,128]{2,0,1:T(8,128)(2,1)}), bf16[48,8,128]{2,0,1:T(8,128)(2,1)S(1)}, u32[]{:S(2)}, u32[]{:S(2)}) async-start(bf16[48,8,128]{2,0,1:T(8,128)(2,1)} %copy_bitcast_fusion.2), calls=%async_computation | async-start | bytes 196608 | tf_op jit(solution)/shard_map/all_to_all | solution.py:66
  13.2 196.3 %all-gather.2.cloned.1.call-start = ((), (), s32[]{:S(2)}) async-start(), calls=%async_computation.4 | async-start | bytes 12779520 | tf_op jit(solution)/shard_map/all_gather | solution.py:102
  31.4 13.4 %all-to-all-start.2 = ((bf16[48,8,1024]{2,0,1:T(8,128)(2,1)}), bf16[48,8,1024]{2,0,1:T(8,128)(2,1)S(1)}, u32[]{:S(2)}, u32[]{:S(2)}) async-start(bf16[48,8,1024]{2,0,1:T(8,128)(2,1)} %bitcast.134), calls=%async_computation.2 | async-start | bytes 1572864 | tf_op jit(solution)/shard_map/all_to_all | solution.py:65
Sparse Core Ops, SparseCore 0:
  29.4 180.0 all-gather.1
where the time goes:
time: 346 us
  waiting for transfers between devices  172 us (50%)
  blocking collectives  71.1 us (21%)
  local copies, waits for them, and re-layouts  30.8 us (9%)
  matrix products  30 us (9%)
  other arithmetic  16.8 us (5%)
  between operations  15.6 us (5%)
  starting transfers between devices  8.69 us (3%)
    all_gather x1, waiting for transfers between devices, per_device(): lax.all_gather(kv_pairs[None], 'seq', axis=0, tiled=True)  163 us
    all_to_all x1, blocking collectives, per_device(): lax.all_to_all(attended_local, 'head', split_axis=0, concat_axis=1, tiled...  62.2 us
    dot_general x1, matrix products, per_device(): jnp.einsum('jnb,nbrjc->nrjc', onehot, lax.all_gather(kv_pairs[None], 'seq...  17.6 us
    gather x6, local copies, waits for them, and re-layouts, step_once(): jnp.take(kv_table, location, axis=0).reshape(STEP * BLOCK, 2 * HEAD_DIM)  16.9 us
    all_to_all x1, blocking collectives, per_device(): lax.all_to_all(values, 'head', split_axis=1, concat_axis=0, tiled=True)  8.93 us
    dot_general x6, matrix products, step_once(): jnp.einsum('hqk,kd->hqd', weights, value_rows, preferred_element_type=jnp...  7.69 us
  transfers between devices with their start and end apart: 3, of which 3 were waited for; matrix products, arithmetic and copies ran while one was open for 3% of the time, Pallas kernels for 0%

commit v1 on v0

v1 whole, which is shorter than its diff:
```python
import functools
import math

import jax
import jax.numpy as jnp
from jax import lax
from jax.experimental import pallas as pl
from jax.experimental.pallas import tpu as pltpu
from jax.sharding import PartitionSpec as P

HEADS = 64
KV_HEADS = 8
HEAD_DIM = 128
BLOCK = 128
GROUP = 4
RINGED = 3
CORES = 2
HALVES = 2
MESH = pl.DeviceIdType.MESH
OWN, RING, EARLY, CROSS, MATE, MATE_EARLY, MATE_CROSS = range(7)


def gather_kernel(
    shards, heads, q_ref, k_ref, v_ref, qo_ref, tab_ref, kv_send, kv_recv, q_send, q_recv, send, recv, local
):
    rows = k_ref.shape[0]
    per_shard = tab_ref.shape[2]
    q_cols = q_ref.shape[1] // heads
    depth = shards // (CORES * HALVES)
    far = depth // 2
    early_rows = RINGED * per_shard // 3
    s = lax.axis_index("seq")
    h = lax.axis_index("head")
    core = s % CORES
    z = (s // CORES) % depth
    half = s // (CORES * depth)

    def seq_at(half_at, z_at):
        return (half_at * depth + z_at) * CORES + core

    up = seq_at(half, (z + 1) % depth)
    down = seq_at(half, (z + depth - 1) % depth)
    mate = s + 1 - 2 * core
    across = seq_at(1 - half, z)
    here = pl.ds(pl.multiple_of(h * rows, 16), rows)

    barrier = pltpu.get_barrier_semaphore()
    for d in range(1, heads):
        pl.semaphore_signal(barrier, inc=1, device_id=(s, (h + d) % heads), device_id_type=MESH)
    for other in (up, down, mate, across):
        pl.semaphore_signal(barrier, inc=1, device_id=(other, h), device_id_type=MESH)
    pl.semaphore_wait(barrier, heads + 3)

    def remote(src, dst, send_sem, recv_sem, to):
        return pltpu.make_async_remote_copy(
            src_ref=src, dst_ref=dst, send_sem=send_sem, recv_sem=recv_sem, device_id=to, device_id_type=MESH
        )

    kv_copies, q_copies = [], []
    for d in range(1, heads):
        peer = (h + d) % heads
        cols = pl.ds(pl.multiple_of(peer * HEAD_DIM, HEAD_DIM), HEAD_DIM)
        for i, ref in enumerate((k_ref, v_ref)):
            kv_copies.append(
                remote(ref.at[:, cols], tab_ref.at[s, i, here], kv_send.at[i, d], kv_recv.at[i, d], (s, peer))
            )
        wide = pl.ds(pl.multiple_of(peer * q_cols, HEAD_DIM), q_cols)
        q_copies.append(remote(q_ref.at[:, wide], qo_ref.at[here], q_send.at[d], q_recv.at[d], (s, peer)))
    cols = pl.ds(pl.multiple_of(h * HEAD_DIM, HEAD_DIM), HEAD_DIM)
    wide = pl.ds(pl.multiple_of(h * q_cols, HEAD_DIM), q_cols)
    kv_local = [
        pltpu.make_async_copy(ref.at[:, cols], tab_ref.at[s, i, here], local.at[i])
        for i, ref in enumerate((k_ref, v_ref))
    ]
    q_local = pltpu.make_async_copy(q_ref.at[:, wide], qo_ref.at[here], local.at[2])
    for copy in kv_copies + kv_local:
        copy.start()
    for copy in kv_local:
        copy.wait()
    for copy in kv_copies:
        copy.wait_recv()

    def flow(mine):
        sent = []

        def chunk(half_at, way, t):
            z_at = (z - t + depth) % depth if way == 0 else (z + t) % depth
            return seq_at(half_at, z_at)

        def piece(kind, way, t):
            late = per_shard - early_rows
            if kind in (RING, MATE):
                at = chunk(mine, way, t)
                return tab_ref.at[at, way] if t == far else tab_ref.at[at]
            at = chunk(0, way, t)
            span = pl.ds(0, early_rows) if kind in (EARLY, MATE_EARLY, OWN) else pl.ds(early_rows, late)
            return tab_ref.at[at, way, span] if t == far else tab_ref.at[at, :, span]

        def copy_of(kind, way, t):
            to = {RING: (up, down)[way], EARLY: (up, down)[way], OWN: across, CROSS: across}.get(kind, mate)
            slot = t + 1 if kind in (RING, EARLY) else t
            if slot == far and kind in (RING, EARLY):
                at = chunk(mine if kind == RING else 0, way, t)
                ref = tab_ref.at[at, way] if kind == RING else tab_ref.at[at, way, pl.ds(0, early_rows)]
            else:
                ref = piece(kind, way, t)
            return remote(ref, ref, send.at[kind, way, slot], recv.at[kind, way, slot], (to, h))

        def go(kind, way, t):
            copy = copy_of(kind, way, t)
            copy.start()
            sent.append(copy)

        def arrive(kind, way, slot):
            if kind in (RING, EARLY):
                half_at = mine if kind == RING else 0
                at = chunk(half_at, way, slot)
                if kind == RING:
                    ref = tab_ref.at[at, way] if slot == far else tab_ref.at[at]
                else:
                    span = pl.ds(0, early_rows)
                    ref = tab_ref.at[at, way, span] if slot == far else tab_ref.at[at, :, span]
                to = (up, down)[way]
            elif kind in (MATE, MATE_EARLY, MATE_CROSS):
                z_at = (z - slot + depth) % depth if way == 0 else (z + slot) % depth
                at = (((mine if kind == MATE else 0) * depth + z_at) * CORES) + 1 - core
                span = pl.ds(0, early_rows) if kind == MATE_EARLY else pl.ds(early_rows, per_shard - early_rows)
                if kind == MATE:
                    ref = tab_ref.at[at, way] if slot == far else tab_ref.at[at]
                else:
                    ref = tab_ref.at[at, way, span] if slot == far else tab_ref.at[at, :, span]
                to = mate
            else:
                ref = piece(kind, way, slot)
                to = across
            remote(ref, ref, send.at[kind, way, slot], recv.at[kind, way, slot], (to, h)).wait_recv()

        crossing = early_rows < per_shard
        stages = [(0, 0)] + [(t, way) for t in range(1, far + 1) for way in (0, 1)]
        for way in (0, 1):
            go(RING, way, 0)
        if mine == 0:
            go(OWN, 0, 0)
        go(MATE, 0, 0)
        if mine == 0 and crossing:
            go(CROSS, 0, 0)
        for copy in q_copies + [q_local]:
            copy.start()
        if mine == 1:
            arrive(OWN, 0, 0)
            for way in (0, 1):
                go(EARLY, way, 0)
            go(MATE_EARLY, 0, 0)
        pending = [(0, 0)]
        for t in range(1, far + 1):
            for way in (0, 1):
                arrive(RING, way, t)
                if t < far:
                    go(RING, way, t)
                go(MATE, way, t)
                if mine == 0 and crossing:
                    go(CROSS, way, t)
            if mine == 1:
                for way in (0, 1):
                    arrive(EARLY, way, t)
                    if t < far:
                        go(EARLY, way, t)
                    go(MATE_EARLY, way, t)
                if crossing:
                    while pending and pending[0][0] < t - 1:
                        at_t, at_way = pending.pop(0)
                        arrive(CROSS, at_way, at_t)
                        go(MATE_CROSS, at_way, at_t)
                    pending += [(t, 0), (t, 1)]
        if mine == 1 and crossing:
            for at_t, at_way in pending:
                arrive(CROSS, at_way, at_t)
                go(MATE_CROSS, at_way, at_t)
        for t, way in stages:
            arrive(MATE, way, t)
            if mine == 1:
                arrive(MATE_EARLY, way, t)
                if crossing:
                    arrive(MATE_CROSS, way, t)
        for copy in sent:
            copy.wait_send()

    @pl.when(half == 0)
    def _():
        flow(0)

    @pl.when(half == 1)
    def _():
        flow(1)

    for copy in kv_copies:
        copy.wait_send()
    q_local.wait()
    for copy in q_copies:
        copy.wait()


def gather(queries, keys, values, shards, heads):
    rows = queries.shape[0]
    depth = shards // (CORES * HALVES)
    far = depth // 2
    anywhere = pl.BlockSpec(memory_space=pl.ANY)
    dma = pltpu.SemaphoreType.DMA
    return pl.pallas_call(
        functools.partial(gather_kernel, shards, heads),
        out_shape=(
            jax.ShapeDtypeStruct((rows * heads, queries.shape[1] // heads), jnp.bfloat16),
            jax.ShapeDtypeStruct((shards, 2, rows * heads, HEAD_DIM), jnp.bfloat16),
        ),
        in_specs=[anywhere] * 3,
        out_specs=(anywhere, anywhere),
        scratch_shapes=[
            dma((2, heads)),
            dma((2, heads)),
            dma((heads,)),
            dma((heads,)),
            dma((7, 2, far + 1)),
            dma((7, 2, far + 1)),
            dma((3,)),
        ],
        compiler_params=pltpu.CompilerParams(collective_id=0, has_side_effects=True),
    )(queries, keys, values)


def attend_kernel(list_ref, count_ref, q_ref, tab_ref, o_ref, kv_ref, m_ref, acc_ref, sems):
    blocks = q_ref.shape[0] // BLOCK
    per_kv = q_ref.shape[1] // HEAD_DIM
    width = list_ref.shape[1]
    scale = math.log2(math.e) / math.sqrt(HEAD_DIM)
    first = lax.axis_index("seq") * blocks

    def groups_of(b):
        return (count_ref[b] + GROUP - 1) // GROUP

    def block_copy(b, j):
        entry = jnp.where(j < count_ref[b], list_ref[b, j], first)
        rows = pl.ds(pl.multiple_of((entry % blocks) * BLOCK, BLOCK), BLOCK)
        return pltpu.make_async_copy(tab_ref.at[entry // blocks, :, rows], kv_ref.at[b, j], sems.at[b, j])

    for b in range(blocks):

        @pl.loop(0, groups_of(b) * GROUP)
        def _(j):
            block_copy(b, j).start()

    @pl.loop(0, blocks)
    def _(b):
        m_ref[...] = jnp.full(m_ref.shape, -1e30, jnp.float32)
        acc_ref[...] = jnp.zeros(acc_ref.shape, jnp.float32)
        query_rows = pl.ds(pl.multiple_of(b * BLOCK, BLOCK), BLOCK)
        count = count_ref[b]

        def update(g, masked):
            k = kv_ref[b, pl.ds(g * GROUP, GROUP), 0].reshape(GROUP * BLOCK, HEAD_DIM)
            v = kv_ref[b, pl.ds(g * GROUP, GROUP), 1].reshape(GROUP * BLOCK, HEAD_DIM)
            v = jnp.concatenate([v, jnp.ones_like(v)], axis=1)
            if masked:
                row = lax.broadcasted_iota(jnp.int32, (BLOCK, BLOCK), 0)
                col = lax.broadcasted_iota(jnp.int32, (BLOCK, BLOCK), 1)
                limits = []
                for i in range(GROUP):
                    j = g * GROUP + i
                    own = list_ref[b, j] == first + b
                    limit = jnp.where(own, row, jnp.full_like(row, BLOCK))
                    limits.append(jnp.where(j < count, limit, jnp.full_like(row, -1)) >= col)
                allowed = jnp.concatenate([limit.astype(jnp.int32) for limit in limits], axis=1) > 0
            for head in range(per_kv):
                q = q_ref[query_rows, pl.ds(head * HEAD_DIM, HEAD_DIM)]
                scores = lax.dot_general(
                    q, k, (((1,), (1,)), ((), ())), preferred_element_type=jnp.float32
                )
                if masked:
                    scores = jnp.where(allowed, scores, jnp.float32(-1e30))
                before = m_ref[head][:, :1]
                newest = jnp.maximum(before, jnp.max(scores, axis=1, keepdims=True))
                prob = jnp.exp2(scores * scale - newest * scale)
                rescale = jnp.exp2(before * scale - newest * scale)
                acc_ref[head] = acc_ref[head] * rescale + jnp.dot(
                    prob.astype(jnp.bfloat16), v, preferred_element_type=jnp.float32
                )
                m_ref[head] = jnp.broadcast_to(newest, (BLOCK, BLOCK))

        @pl.loop(0, groups_of(b))
        def _(g):
            masked = (g + 1) * GROUP > count
            for i in range(GROUP):
                j = g * GROUP + i
                block_copy(b, j).wait()
                masked = masked | (list_ref[b, j] == first + b)

            @pl.when(masked)
            def _():
                update(g, True)

            @pl.when(jnp.logical_not(masked))
            def _():
                update(g, False)

        for head in range(per_kv):
            acc = acc_ref[head]
            o_ref[query_rows, pl.ds(head * HEAD_DIM, HEAD_DIM)] = (
                acc[:, :HEAD_DIM] / acc[:, HEAD_DIM:]
            ).astype(jnp.bfloat16)


def attend(entries, counts, queries, table):
    blocks = queries.shape[0] // BLOCK
    per_kv = queries.shape[1] // HEAD_DIM
    width = entries.shape[1]
    whole = pl.BlockSpec(memory_space=pltpu.VMEM)
    scalars = pl.BlockSpec(memory_space=pltpu.SMEM)
    return pl.pallas_call(
        attend_kernel,
        out_shape=jax.ShapeDtypeStruct(queries.shape, jnp.bfloat16),
        in_specs=[scalars, scalars, whole, pl.BlockSpec(memory_space=pl.ANY)],
        out_specs=whole,
        scratch_shapes=[
            pltpu.VMEM((blocks, width, 2, BLOCK, HEAD_DIM), jnp.bfloat16),
            pltpu.VMEM((per_kv, BLOCK, BLOCK), jnp.float32),
            pltpu.VMEM((per_kv, BLOCK, 2 * HEAD_DIM), jnp.float32),
            pltpu.SemaphoreType.DMA((blocks, width)),
        ],
        compiler_params=pltpu.CompilerParams(vmem_limit_bytes=40 * 1024 * 1024),
    )(entries, counts, queries, table)


def return_kernel(heads, o_ref, out_ref, send, recv, local):
    rows = out_ref.shape[0]
    cols = o_ref.shape[1]
    s = lax.axis_index("seq")
    h = lax.axis_index("head")
    barrier = pltpu.get_barrier_semaphore()
    for d in range(1, heads):
        pl.semaphore_signal(barrier, inc=1, device_id=(s, (h + d) % heads), device_id_type=MESH)
    pl.semaphore_wait(barrier, heads - 1)
    mine = pl.ds(pl.multiple_of(h * cols, HEAD_DIM), cols)
    copies = []
    for d in range(1, heads):
        peer = (h + d) % heads
        copies.append(
            pltpu.make_async_remote_copy(
                src_ref=o_ref.at[pl.ds(pl.multiple_of(peer * rows, 16), rows)],
                dst_ref=out_ref.at[:, mine],
                send_sem=send.at[d],
                recv_sem=recv.at[d],
                device_id=(s, peer),
                device_id_type=MESH,
            )
        )
    own = pltpu.make_async_copy(
        o_ref.at[pl.ds(pl.multiple_of(h * rows, 16), rows)], out_ref.at[:, mine], local
    )
    for copy in copies + [own]:
        copy.start()
    for copy in copies + [own]:
        copy.wait()


def give_back(attended, heads):
    rows, cols = attended.shape
    anywhere = pl.BlockSpec(memory_space=pl.ANY)
    return pl.pallas_call(
        functools.partial(return_kernel, heads),
        out_shape=jax.ShapeDtypeStruct((rows // heads, cols * heads), jnp.bfloat16),
        in_specs=[anywhere],
        out_specs=anywhere,
        scratch_shapes=[
            pltpu.SemaphoreType.DMA((heads,)),
            pltpu.SemaphoreType.DMA((heads,)),
            pltpu.SemaphoreType.DMA,
        ],
        compiler_params=pltpu.CompilerParams(collective_id=1, has_side_effects=True),
    )(attended)


def per_device(queries, keys, values, block_list, block_count):
    shards = lax.axis_size("seq")
    heads = lax.axis_size("head")
    blocks = block_list.shape[1] // shards
    s = lax.axis_index("seq")
    h = lax.axis_index("head")
    width = block_list.shape[2]
    entries = lax.dynamic_slice(block_list, (h, s * blocks, 0), (1, blocks, width))[0]
    counts = lax.dynamic_slice(block_count, (h, s * blocks), (1, blocks))[0]
    query_local, table = gather(queries, keys, values, shards, heads)
    attended = attend(entries, counts, query_local, table)
    return give_back(attended, heads)


def solution(mesh):
    placed = (
        P(("seq", "head"), None),
        P(("seq", "head"), None),
        P(("seq", "head"), None),
        P(),
        P(),
    )
    return jax.shard_map(
        per_device, mesh=mesh, in_specs=placed, out_specs=P(("seq", "head"), None), check_vma=False
    )
```

time: 346 us -> 171 us (0.49)
  the two profiles are of different devices: /device:TPU:4 before, /device:TPU:30 now
where the time goes in v1:
time: 171 us
  Pallas kernels  161 us (94%)
  local copies, waits for them, and re-layouts  9.76 us (6%)
    pallas_call x1, Pallas kernels, gather(): pl.pallas_call(functools.partial(gather_kernel, shards, heads), out_shape...  87.7 us
    pallas_call x1, Pallas kernels, give_back(): pl.pallas_call(functools.partial(return_kernel, heads), out_shape=jax.Sha...  50.8 us
    pallas_call x1, Pallas kernels, attend(): pl.pallas_call(attend_kernel, out_shape=jax.ShapeDtypeStruct(queries.shap...  22.9 us
    unnamed x9, local copies, waits for them, and re-layouts  8.79 us

profile of v1, /device:TPU:30, one launch (start us, length us, event | category | flops | bytes accessed | tf_op | source)
XLA Modules:
  0.0 171.1 jit_solution(11073068744872060107)
XLA Ops:
  0.0 0.0 copy-start
  0.0 0.8 dynamic-slice_bitcast_fusion.count_ref
  0.8 0.2 copy-done
  1.0 0.1 constant_dynamic-slice_fusion
  1.0 0.1 copy.6
  1.1 87.7 %shard_map.55 = (bf16[384,1024]{1,0:T(8,128)(2,1)}, bf16[64,2,384,128]{3,2,1,0:T(8,128)(2,1)}) custom-call(bf16[48,8192]{1,0:T(8,128)(2,1)} %q_ref.1, bf16[48,1024]{1,0:T(8,128)(2,1)} %k_ref.1, bf16[48,1024]{1,0:T(8,128)(2,1)} %v_ref.1), custom_call_target="tpu_custom_call" | custom-call | tf_op jit(solution)/shard_map/pallas_call | solution.py:209
  88.8 0.0 copy-start.1
  88.8 4.6 %copy-done.1 = bf16[64,2,384,128]{3,2,1,0:T(8,128)(2,1)S(1)} copy-done((bf16[64,2,384,128]{3,2,1,0:T(8,128)(2,1)S(1)}, bf16[64,2,384,128]{3,2,1,0:T(8,128)(2,1)}, u32[]{:S(2)}) %copy-start.1) | copy-done | bytes 12582936
  93.4 0.0 copy-start.3
  93.4 1.1 copy-done.3
  94.5 22.9 %shard_map.56.o_ref = bf16[384,1024]{1,0:T(8,128)(2,1)S(1)} custom-call(s32[3,32]{1,0:T(4,128)S(1)} %bitcast.3, s32[3]{0:T(128)S(1)} %dynamic-slice_bitcast_fusion.count_ref, bf16[384,1024]{1,0:T(8,128)(2,1)S(1)} %copy-done.3, bf16[64,2,384,128]{3,2,1,0:T(8,128)(2,1)S(1)} %copy-done.1), custom_call_target="tpu_custom_call" | custom-call | tf_op jit(solution)/shard_map/pallas_call | solution.py:317
  117.4 0.0 copy-start.2
  117.4 0.9 copy-done.2
  118.2 50.8 %shard_map.57 = bf16[48,8192]{1,0:T(8,128)(2,1)} custom-call(bf16[384,1024]{1,0:T(8,128)(2,1)} %copy-done.2), custom_call_target="tpu_custom_call" | custom-call | tf_op jit(solution)/shard_map/pallas_call | solution.py:367
  169.1 2.1 %copy.8 = bf16[48,8192]{1,0:T(8,128)(2,1)} copy(bf16[48,8192]{1,0:T(8,128)(2,1)} %shard_map.57) | data formatting | bytes 1572864
Async XLA Ops:
  0.0 1.0 copy-start
  88.8 4.6 %copy-start.1 = (bf16[64,2,384,128]{3,2,1,0:T(8,128)(2,1)S(1)}, bf16[64,2,384,128]{3,2,1,0:T(8,128)(2,1)}, u32[]{:S(2)}) copy-start(bf16[64,2,384,128]{3,2,1,0:T(8,128)(2,1)} %get-tuple-element.8.tab_ref) | copy-start | bytes 37748740
  93.4 1.1 copy-start.3
  117.4 0.9 copy-start.2

commit v2 on v1

v2 whole, which is shorter than its diff:
```python
import functools
import math

import jax
import jax.numpy as jnp
from jax import lax
from jax.experimental import pallas as pl
from jax.experimental.pallas import tpu as pltpu
from jax.sharding import PartitionSpec as P

HEADS = 64
KV_HEADS = 8
HEAD_DIM = 128
BLOCK = 128
GROUP = 8
EARLY_PART = (10, 24)
LAG = 2
CORES = 2
HALVES = 2
MESH = pl.DeviceIdType.MESH
OWN, RING, EARLY, CROSS, MATE, MATE_EARLY, MATE_CROSS = range(7)


def gather_kernel(
    shards, heads, q_ref, k_ref, v_ref, qo_ref, tab_ref, kv_send, kv_recv, q_send, q_recv, send, recv, local
):
    rows = k_ref.shape[0]
    per_shard = tab_ref.shape[2]
    q_cols = q_ref.shape[1] // heads
    depth = shards // (CORES * HALVES)
    far = depth // 2
    early_rows = per_shard * EARLY_PART[0] // EARLY_PART[1]
    s = lax.axis_index("seq")
    h = lax.axis_index("head")
    core = s % CORES
    z = (s // CORES) % depth
    half = s // (CORES * depth)

    def seq_at(half_at, z_at):
        return (half_at * depth + z_at) * CORES + core

    up = seq_at(half, (z + 1) % depth)
    down = seq_at(half, (z + depth - 1) % depth)
    mate = s + 1 - 2 * core
    across = seq_at(1 - half, z)
    here = pl.ds(pl.multiple_of(h * rows, 16), rows)

    barrier = pltpu.get_barrier_semaphore()
    for d in range(1, heads):
        pl.semaphore_signal(barrier, inc=1, device_id=(s, (h + d) % heads), device_id_type=MESH)
    for other in (up, down, mate, across):
        pl.semaphore_signal(barrier, inc=1, device_id=(other, h), device_id_type=MESH)
    pl.semaphore_wait(barrier, heads + 3)

    def remote(src, dst, send_sem, recv_sem, to):
        return pltpu.make_async_remote_copy(
            src_ref=src, dst_ref=dst, send_sem=send_sem, recv_sem=recv_sem, device_id=to, device_id_type=MESH
        )

    kv_copies, q_copies = [], []
    for d in range(1, heads):
        peer = (h + d) % heads
        cols = pl.ds(pl.multiple_of(peer * HEAD_DIM, HEAD_DIM), HEAD_DIM)
        for i, ref in enumerate((k_ref, v_ref)):
            kv_copies.append(
                remote(ref.at[:, cols], tab_ref.at[s, i, here], kv_send.at[i, d], kv_recv.at[i, d], (s, peer))
            )
        wide = pl.ds(pl.multiple_of(peer * q_cols, HEAD_DIM), q_cols)
        q_copies.append(remote(q_ref.at[:, wide], qo_ref.at[here], q_send.at[d], q_recv.at[d], (s, peer)))
    cols = pl.ds(pl.multiple_of(h * HEAD_DIM, HEAD_DIM), HEAD_DIM)
    wide = pl.ds(pl.multiple_of(h * q_cols, HEAD_DIM), q_cols)
    kv_local = [
        pltpu.make_async_copy(ref.at[:, cols], tab_ref.at[s, i, here], local.at[i])
        for i, ref in enumerate((k_ref, v_ref))
    ]
    q_local = pltpu.make_async_copy(q_ref.at[:, wide], qo_ref.at[here], local.at[2])
    for copy in kv_copies + kv_local:
        copy.start()
    for copy in kv_local:
        copy.wait()
    for copy in kv_copies:
        copy.wait_recv()

    def flow(mine):
        sent = []

        def copy_of(kind, way, slot, hops, other=False):
            z_at = (z - hops + depth) % depth if way == 0 else (z + hops) % depth
            half_at = mine if kind in (RING, MATE) else 0
            at = (half_at * depth + z_at) * CORES + (1 - core if other else core)
            if kind in (EARLY, MATE_EARLY, OWN):
                span = pl.ds(0, early_rows)
            elif kind in (CROSS, MATE_CROSS):
                span = pl.ds(early_rows, per_shard - early_rows)
            else:
                span = pl.ds(0, per_shard)
            ref = tab_ref.at[at, way, span] if slot == far else tab_ref.at[at, :, span]
            to = {RING: (up, down)[way], EARLY: (up, down)[way], OWN: across, CROSS: across}.get(kind, mate)
            return remote(ref, ref, send.at[kind, way, slot], recv.at[kind, way, slot], (to, h))

        def go(kind, way, hops):
            copy = copy_of(kind, way, hops + 1 if kind in (RING, EARLY) else hops, hops)
            copy.start()
            sent.append(copy)

        def arrive(kind, way, slot):
            copy_of(kind, way, slot, slot, kind in (MATE, MATE_EARLY, MATE_CROSS)).wait_recv()

        stages = [(0, 0)] + [(t, way) for t in range(1, far + 1) for way in (0, 1)]
        for way in (0, 1):
            go(RING, way, 0)
        if mine == 0:
            go(OWN, 0, 0)
            go(CROSS, 0, 0)
        go(MATE, 0, 0)
        for copy in q_copies + [q_local]:
            copy.start()
        if mine == 1:
            arrive(OWN, 0, 0)
            for way in (0, 1):
                go(EARLY, way, 0)
            go(MATE_EARLY, 0, 0)
        pending = [(0, 0)]
        for t in range(1, far + 1):
            for way in (0, 1):
                arrive(RING, way, t)
                if t < far:
                    go(RING, way, t)
            if mine == 1:
                for way in (0, 1):
                    arrive(EARLY, way, t)
                    if t < far:
                        go(EARLY, way, t)
            for way in (0, 1):
                if mine == 0:
                    go(CROSS, way, t)
                go(MATE, way, t)
                if mine == 1:
                    go(MATE_EARLY, way, t)
            if mine == 1:
                while pending and pending[0][0] < t - LAG:
                    at_t, at_way = pending.pop(0)
                    arrive(CROSS, at_way, at_t)
                    go(MATE_CROSS, at_way, at_t)
                pending += [(t, 0), (t, 1)]
        if mine == 1:
            for at_t, at_way in pending:
                arrive(CROSS, at_way, at_t)
                go(MATE_CROSS, at_way, at_t)
        for t, way in stages:
            arrive(MATE, way, t)
            if mine == 1:
                arrive(MATE_EARLY, way, t)
                arrive(MATE_CROSS, way, t)
        for copy in sent:
            copy.wait_send()

    @pl.when(half == 0)
    def _():
        flow(0)

    @pl.when(half == 1)
    def _():
        flow(1)

    for copy in kv_copies:
        copy.wait_send()
    q_local.wait()
    for copy in q_copies:
        copy.wait()


def gather(queries, keys, values, shards, heads):
    rows = queries.shape[0]
    depth = shards // (CORES * HALVES)
    far = depth // 2
    in_hbm = pl.BlockSpec(memory_space=pltpu.HBM)
    dma = pltpu.SemaphoreType.DMA
    return pl.pallas_call(
        functools.partial(gather_kernel, shards, heads),
        out_shape=(
            jax.ShapeDtypeStruct((rows * heads, queries.shape[1] // heads), jnp.bfloat16),
            jax.ShapeDtypeStruct((shards, 2, rows * heads, HEAD_DIM), jnp.bfloat16),
        ),
        in_specs=[in_hbm] * 3,
        out_specs=(pl.BlockSpec(memory_space=pltpu.VMEM),) * 2,
        scratch_shapes=[
            dma((2, heads)),
            dma((2, heads)),
            dma((heads,)),
            dma((heads,)),
            dma((7, 2, far + 1)),
            dma((7, 2, far + 1)),
            dma((3,)),
        ],
        compiler_params=pltpu.CompilerParams(collective_id=0, has_side_effects=True, vmem_limit_bytes=24 * 1024 * 1024),
    )(queries, keys, values)


def attend_kernel(list_ref, count_ref, q_ref, tab_ref, o_ref, qt_ref, m_ref, acc_ref):
    blocks = q_ref.shape[0] // BLOCK
    per_kv = q_ref.shape[1] // HEAD_DIM
    scale = math.log2(math.e) / math.sqrt(HEAD_DIM)
    first = lax.axis_index("seq") * blocks

    def head_cols(head):
        return pl.ds(head * HEAD_DIM, HEAD_DIM)

    @pl.loop(0, blocks)
    def _(b):
        query_rows = pl.ds(pl.multiple_of(b * BLOCK, BLOCK), BLOCK)
        count = count_ref[b]
        groups = (count + GROUP - 1) // GROUP
        for head in range(per_kv):
            qt_ref[:, head * BLOCK : (head + 1) * BLOCK] = q_ref[query_rows, head_cols(head)].T
        m_ref[...] = jnp.full(m_ref.shape, -1e30, jnp.float32)
        acc_ref[...] = jnp.zeros(acc_ref.shape, jnp.float32)

        def listed(g, i):
            parts = []
            for j in range(GROUP):
                at = g * GROUP + j
                entry = jnp.where(at < count, list_ref[b, at], first)
                rows = pl.ds(pl.multiple_of((entry % blocks) * BLOCK, BLOCK), BLOCK)
                parts.append(tab_ref[entry // blocks, i, rows])
            return jnp.concatenate(parts, axis=0)

        def update(g, masked):
            k = listed(g, 0)
            v = listed(g, 1)
            vt = jnp.concatenate([v.T, jnp.ones((16, GROUP * BLOCK), v.dtype)], axis=0)
            scores = jnp.dot(k, qt_ref[...], preferred_element_type=jnp.float32)
            if masked:
                row = lax.broadcasted_iota(jnp.int32, (BLOCK, BLOCK), 1)
                col = lax.broadcasted_iota(jnp.int32, (BLOCK, BLOCK), 0)
                limits = []
                for j in range(GROUP):
                    at = g * GROUP + j
                    limit = jnp.where(list_ref[b, at] == first + b, row, jnp.full_like(row, BLOCK))
                    limit = jnp.where(at < count, limit, jnp.full_like(row, -1))
                    limits.append((limit >= col).astype(jnp.int32))
                allowed = jnp.concatenate(limits, axis=0) > 0
                allowed = jnp.concatenate([allowed] * per_kv, axis=1)
                scores = jnp.where(allowed, scores, jnp.float32(-1e30))
            before = m_ref[:1]
            newest = jnp.maximum(before, jnp.max(scores, axis=0, keepdims=True))
            prob = jnp.exp2(scores * scale - newest * scale).astype(jnp.bfloat16)
            rescale = jnp.exp2(before * scale - newest * scale)
            acc_ref[...] = acc_ref[...] * rescale + jnp.dot(vt, prob, preferred_element_type=jnp.float32)
            m_ref[:1] = newest

        @pl.loop(0, groups)
        def _(g):
            masked = (g + 1) * GROUP > count
            for j in range(GROUP):
                masked = masked | (list_ref[b, g * GROUP + j] == first + b)

            @pl.when(masked)
            def _():
                update(g, True)

            @pl.when(jnp.logical_not(masked))
            def _():
                update(g, False)

        for head in range(per_kv):
            acc = acc_ref[:, head * BLOCK : (head + 1) * BLOCK]
            out = acc[:HEAD_DIM] / acc[HEAD_DIM : HEAD_DIM + 1]
            o_ref[query_rows, head_cols(head)] = out.T.astype(jnp.bfloat16)


def attend(entries, counts, queries, table):
    per_kv = queries.shape[1] // HEAD_DIM
    whole = pl.BlockSpec(memory_space=pltpu.VMEM)
    scalars = pl.BlockSpec(memory_space=pltpu.SMEM)
    return pl.pallas_call(
        attend_kernel,
        out_shape=jax.ShapeDtypeStruct(queries.shape, jnp.bfloat16),
        in_specs=[scalars, scalars, whole, whole],
        out_specs=whole,
        scratch_shapes=[
            pltpu.VMEM((HEAD_DIM, per_kv * BLOCK), jnp.bfloat16),
            pltpu.VMEM((8, per_kv * BLOCK), jnp.float32),
            pltpu.VMEM((HEAD_DIM + 16, per_kv * BLOCK), jnp.float32),
        ],
        compiler_params=pltpu.CompilerParams(vmem_limit_bytes=30 * 1024 * 1024),
    )(entries, counts, queries, table)


def return_kernel(heads, o_ref, out_ref, send, recv, local):
    rows = out_ref.shape[0]
    cols = o_ref.shape[1]
    s = lax.axis_index("seq")
    h = lax.axis_index("head")
    barrier = pltpu.get_barrier_semaphore()
    for d in range(1, heads):
        pl.semaphore_signal(barrier, inc=1, device_id=(s, (h + d) % heads), device_id_type=MESH)
    pl.semaphore_wait(barrier, heads - 1)
    mine = pl.ds(pl.multiple_of(h * cols, HEAD_DIM), cols)
    copies = []
    for d in range(1, heads):
        peer = (h + d) % heads
        copies.append(
            pltpu.make_async_remote_copy(
                src_ref=o_ref.at[pl.ds(pl.multiple_of(peer * rows, 16), rows)],
                dst_ref=out_ref.at[:, mine],
                send_sem=send.at[d],
                recv_sem=recv.at[d],
                device_id=(s, peer),
                device_id_type=MESH,
            )
        )
    own = pltpu.make_async_copy(
        o_ref.at[pl.ds(pl.multiple_of(h * rows, 16), rows)], out_ref.at[:, mine], local
    )
    for copy in copies + [own]:
        copy.start()
    for copy in copies + [own]:
        copy.wait()


def give_back(attended, heads):
    rows, cols = attended.shape
    anywhere = pl.BlockSpec(memory_space=pl.ANY)
    return pl.pallas_call(
        functools.partial(return_kernel, heads),
        out_shape=jax.ShapeDtypeStruct((rows // heads, cols * heads), jnp.bfloat16),
        in_specs=[anywhere],
        out_specs=anywhere,
        scratch_shapes=[
            pltpu.SemaphoreType.DMA((heads,)),
            pltpu.SemaphoreType.DMA((heads,)),
            pltpu.SemaphoreType.DMA,
        ],
        compiler_params=pltpu.CompilerParams(collective_id=1, has_side_effects=True, vmem_limit_bytes=1024 * 1024),
    )(attended)


def per_device(queries, keys, values, block_list, block_count):
    shards = lax.axis_size("seq")
    heads = lax.axis_size("head")
    blocks = block_list.shape[1] // shards
    s = lax.axis_index("seq")
    h = lax.axis_index("head")
    width = block_list.shape[2]
    entries = lax.dynamic_slice(block_list, (h, s * blocks, 0), (1, blocks, width))[0]
    counts = lax.dynamic_slice(block_count, (h, s * blocks), (1, blocks))[0]
    query_local, table = gather(queries, keys, values, shards, heads)
    attended = attend(entries, counts, query_local, table)
    return give_back(attended, heads)


def solution(mesh):
    placed = (
        P(("seq", "head"), None),
        P(("seq", "head"), None),
        P(("seq", "head"), None),
        P(),
        P(),
    )
    return jax.shard_map(
        per_device, mesh=mesh, in_specs=placed, out_specs=P(("seq", "head"), None), check_vma=False
    )
```

time: 171 us -> 113 us (0.66)
  Pallas kernels: 161 us -> 108 us
  local copies, waits for them, and re-layouts: 9.76 us -> 4.92 us
    pallas_call x1, Pallas kernels: 50.8 us -> 26.7 us  [give_back(): pl.pallas_call(functools.partial(return_kernel, heads), out_shape=jax.Sha...]
    pallas_call x1, Pallas kernels: 87.7 us -> 68.9 us  [gather(): pl.pallas_call(functools.partial(gather_kernel, shards, heads), out_shape...]
    pallas_call x1, Pallas kernels: 22.9 us -> 11.9 us  [attend(): pl.pallas_call(attend_kernel, out_shape=jax.ShapeDtypeStruct(queries.shap...]
    unnamed x9, local copies, waits for them, and re-layouts: 8.79 us -> 3.96 us
where the time goes in v2:
time: 113 us
  Pallas kernels  108 us (96%)
  local copies, waits for them, and re-layouts  4.92 us (4%)
    pallas_call x1, Pallas kernels, gather(): pl.pallas_call(functools.partial(gather_kernel, shards, heads), out_shape...  68.9 us
    pallas_call x1, Pallas kernels, give_back(): pl.pallas_call(functools.partial(return_kernel, heads), out_shape=jax.Sha...  26.7 us
    pallas_call x1, Pallas kernels, attend(): pl.pallas_call(attend_kernel, out_shape=jax.ShapeDtypeStruct(queries.shap...  11.9 us
    unnamed x9, local copies, waits for them, and re-layouts  3.96 us

profile of v2, /device:TPU:30, one launch (start us, length us, event | category | flops | bytes accessed | tf_op | source)
XLA Modules:
  0.0 112.5 jit_solution(9854558721357587243)
XLA Ops:
  0.0 0.0 copy-start
  0.0 0.8 dynamic-slice_bitcast_fusion.count_ref
  0.8 0.2 copy-done
  1.0 0.1 constant_dynamic-slice_fusion
  1.0 0.1 copy.6
  1.1 0.0 copy-start.1
  1.1 1.1 %copy-done.1 = bf16[48,8192]{1,0:T(8,128)(2,1)S(1)} copy-done((bf16[48,8192]{1,0:T(8,128)(2,1)S(1)}, bf16[48,8192]{1,0:T(8,128)(2,1)}, u32[]{:S(2)}) %copy-start.1) | copy-done | bytes 786456
  2.3 0.0 copy-start.2
  2.3 0.9 copy-done.2
  3.2 0.0 copy-start.3
  3.2 0.9 copy-done.3
  4.0 68.9 %shard_map.55 = (bf16[384,1024]{1,0:T(8,128)(2,1)S(1)}, bf16[64,2,384,128]{3,2,1,0:T(8,128)(2,1)S(1)}) custom-call(bf16[48,8192]{1,0:T(8,128)(2,1)S(1)} %copy-done.1, bf16[48,1024]{1,0:T(8,128)(2,1)S(1)} %copy-done.2, bf16[48,1024]{1,0:T(8,128)(2,1)S(1)} %copy-done.3), custom_call_target="tpu_custom_call" | custom-call | tf_op jit(solution)/shard_map/pallas_call | solution.py:179
  73.0 11.9 %shard_map.56.o_ref = bf16[384,1024]{1,0:T(8,128)(2,1)S(1)} custom-call(s32[3,32]{1,0:T(4,128)S(1)} %bitcast.3, s32[3]{0:T(128)S(1)} %dynamic-slice_bitcast_fusion.count_ref, bf16[384,1024]{1,0:T(8,128)(2,1)S(1)} %get-tuple-element.7.q_ref, bf16[64,2,384,128]{3,2,1,0:T(8,128)(2,1)S(1)} %get-tuple-element.8.tab_ref), custom_call_target="tpu_custom_call" | custom-call | tf_op jit(solution)/shard_map/pallas_call | solution.py:276
  84.9 26.7 %shard_map.57 = bf16[48,8192]{1,0:T(8,128)(2,1)S(1)} custom-call(bf16[384,1024]{1,0:T(8,128)(2,1)S(1)} %shard_map.56.o_ref), custom_call_target="tpu_custom_call" | custom-call | tf_op jit(solution)/shard_map/pallas_call | solution.py:325
  111.7 0.9 copy.8
Async XLA Ops:
  0.0 1.0 copy-start
  1.1 1.1 %copy-start.1 = (bf16[48,8192]{1,0:T(8,128)(2,1)S(1)}, bf16[48,8192]{1,0:T(8,128)(2,1)}, u32[]{:S(2)}) copy-start(bf16[48,8192]{1,0:T(8,128)(2,1)} %q_ref.1) | copy-start | bytes 2359300
  2.3 0.9 copy-start.2
  3.2 0.9 copy-start.3

commit v3 on v2

--- a/solution.py
+++ b/solution.py
@@ -13,6 +13,8 @@
 HEAD_DIM = 128
 BLOCK = 128
 GROUP = 8
+CHUNK = 1024
+LARGEST = 2.0**40
 EARLY_PART = (10, 24)
 LAG = 2
 CORES = 2
@@ -98,13 +100,26 @@
             to = {RING: (up, down)[way], EARLY: (up, down)[way], OWN: across, CROSS: across}.get(kind, mate)
             return remote(ref, ref, send.at[kind, way, slot], recv.at[kind, way, slot], (to, h))
 
+        def needed(kind, way, hops):
+            if kind != MATE or hops == 0:
+                return None
+            return z >= hops if way == 0 else z + hops >= depth
+
+        def guarded(when, act):
+            if when is None:
+                act()
+            else:
+                pl.when(when)(act)
+
         def go(kind, way, hops):
             copy = copy_of(kind, way, hops + 1 if kind in (RING, EARLY) else hops, hops)
-            copy.start()
-            sent.append(copy)
+            when = needed(kind, way, hops)
+            guarded(when, copy.start)
+            sent.append((when, copy))
 
         def arrive(kind, way, slot):
-            copy_of(kind, way, slot, slot, kind in (MATE, MATE_EARLY, MATE_CROSS)).wait_recv()
+            copy = copy_of(kind, way, slot, slot, kind in (MATE, MATE_EARLY, MATE_CROSS))
+            guarded(needed(kind, way, slot), copy.wait_recv)
 
         stages = [(0, 0)] + [(t, way) for t in range(1, far + 1) for way in (0, 1)]
         for way in (0, 1):
@@ -152,8 +167,8 @@
             if mine == 1:
                 arrive(MATE_EARLY, way, t)
                 arrive(MATE_CROSS, way, t)
-        for copy in sent:
-            copy.wait_send()
+        for when, copy in sent:
+            guarded(when, copy.wait_send)
 
     @pl.when(half == 0)
     def _():
@@ -200,6 +215,7 @@
 def attend_kernel(list_ref, count_ref, q_ref, tab_ref, o_ref, qt_ref, m_ref, acc_ref):
     blocks = q_ref.shape[0] // BLOCK
     per_kv = q_ref.shape[1] // HEAD_DIM
+    columns = per_kv * BLOCK
     scale = math.log2(math.e) / math.sqrt(HEAD_DIM)
     first = lax.axis_index("seq") * blocks
 
@@ -213,41 +229,63 @@
         groups = (count + GROUP - 1) // GROUP
         for head in range(per_kv):
             qt_ref[:, head * BLOCK : (head + 1) * BLOCK] = q_ref[query_rows, head_cols(head)].T
-        m_ref[...] = jnp.full(m_ref.shape, -1e30, jnp.float32)
-        acc_ref[...] = jnp.zeros(acc_ref.shape, jnp.float32)
-
-        def listed(g, i):
-            parts = []
-            for j in range(GROUP):
-                at = g * GROUP + j
-                entry = jnp.where(at < count, list_ref[b, at], first)
-                rows = pl.ds(pl.multiple_of((entry % blocks) * BLOCK, BLOCK), BLOCK)
-                parts.append(tab_ref[entry // blocks, i, rows])
-            return jnp.concatenate(parts, axis=0)
+
+        def listed(at, i):
+            entry = jnp.where(at < count, list_ref[b, at], first)
+            rows = pl.ds(pl.multiple_of((entry % blocks) * BLOCK, BLOCK), BLOCK)
+            return tab_ref[entry // blocks, i, rows]
+
+        def listed_group(g, i):
+            return jnp.concatenate([listed(g * GROUP + j, i) for j in range(GROUP)], axis=0)
+
+        def allowed(at):
+            row = lax.broadcasted_iota(jnp.int32, (BLOCK, BLOCK), 1)
+            col = lax.broadcasted_iota(jnp.int32, (BLOCK, BLOCK), 0)
+            limit = jnp.where(list_ref[b, at] == first + b, row, jnp.full_like(row, BLOCK))
+            limit = jnp.where(at < count, limit, jnp.full_like(row, -1))
+            return (limit >= col).astype(jnp.int32)
+
+        def allowed_group(g, heads):
+            parts = jnp.concatenate([allowed(g * GROUP + j) for j in range(GROUP)], axis=0)
+            return jnp.concatenate([parts] * heads, axis=1) > 0
+
+        def with_ones(v):
+            return jnp.concatenate([v.T, jnp.ones((16, v.shape[0]), v.dtype)], axis=0)
+
+        scores = jnp.dot(listed(0, 0), qt_ref[...], preferred_element_type=jnp.float32)
+        start = jnp.concatenate([allowed(0)] * per_kv, axis=1) > 0
+        scores = jnp.where(start, scores, jnp.float32(-1e30))
+        m_ref[:1] = jnp.max(scores, axis=0, keepdims=True)
+        acc_ref[0] = jnp.zeros(acc_ref.shape[1:], jnp.float32)
 
         def update(g, masked):
-            k = listed(g, 0)
-            v = listed(g, 1)
-            vt = jnp.concatenate([v.T, jnp.ones((16, GROUP * BLOCK), v.dtype)], axis=0)
-            scores = jnp.dot(k, qt_ref[...], preferred_element_type=jnp.float32)
-            if masked:
-                row = lax.broadcasted_iota(jnp.int32, (BLOCK, BLOCK), 1)
-                col = lax.broadcasted_iota(jnp.int32, (BLOCK, BLOCK), 0)
-                limits = []
-                for j in range(GROUP):
-                    at = g * GROUP + j
-                    limit = jnp.where(list_ref[b, at] == first + b, row, jnp.full_like(row, BLOCK))
-                    limit = jnp.where(at < count, limit, jnp.full_like(row, -1))
-                    limits.append((limit >= col).astype(jnp.int32))
-                allowed = jnp.concatenate(limits, axis=0) > 0
-                allowed = jnp.concatenate([allowed] * per_kv, axis=1)
-                scores = jnp.where(allowed, scores, jnp.float32(-1e30))
-            before = m_ref[:1]
-            newest = jnp.maximum(before, jnp.max(scores, axis=0, keepdims=True))
-            prob = jnp.exp2(scores * scale - newest * scale).astype(jnp.bfloat16)
-            rescale = jnp.exp2(before * scale - newest * scale)
-            acc_ref[...] = acc_ref[...] * rescale + jnp.dot(vt, prob, preferred_element_type=jnp.float32)
-            m_ref[:1] = newest
+            k = listed_group(g, 0)
+            vt = with_ones(listed_group(g, 1))
+            for c in range(columns // CHUNK):
+                cols = pl.ds(c * CHUNK, CHUNK)
+                scores = jnp.dot(k, qt_ref[:, cols], preferred_element_type=jnp.float32)
+                if masked:
+                    scores = jnp.where(allowed_group(g, CHUNK // BLOCK), scores, jnp.float32(-1e30))
+                prob = jnp.exp2(scores * scale - m_ref[:1, cols] * scale).astype(jnp.bfloat16)
+                acc_ref[(g + 1) % 2, :, cols] = acc_ref[g % 2, :, cols] + jnp.dot(
+                    vt, prob, preferred_element_type=jnp.float32
+                )
+
+        def rescaled_update(g):
+            k = listed_group(g, 0)
+            vt = with_ones(listed_group(g, 1))
+            for c in range(columns // CHUNK):
+                cols = pl.ds(c * CHUNK, CHUNK)
+                scores = jnp.dot(k, qt_ref[:, cols], preferred_element_type=jnp.float32)
+                scores = jnp.where(allowed_group(g, CHUNK // BLOCK), scores, jnp.float32(-1e30))
+                before = m_ref[:1, cols]
+                newest = jnp.maximum(before, jnp.max(scores, axis=0, keepdims=True))
+                prob = jnp.exp2(scores * scale - newest * scale).astype(jnp.bfloat16)
+                rescale = jnp.exp2(before * scale - newest * scale)
+                acc_ref[(g + 1) % 2, :, cols] = acc_ref[g % 2, :, cols] * rescale + jnp.dot(
+                    vt, prob, preferred_element_type=jnp.float32
+                )
+                m_ref[:1, cols] = newest
 
         @pl.loop(0, groups)
         def _(g):
@@ -263,8 +301,15 @@
             def _():
                 update(g, False)
 
+            sums = acc_ref[(g + 1) % 2, HEAD_DIM : HEAD_DIM + 1]
+            fits = jnp.min(jnp.where(sums < LARGEST, 1.0, 0.0)) > 0.5
+
+            @pl.when(jnp.logical_not(fits))
+            def _():
+                rescaled_update(g)
+
         for head in range(per_kv):
-            acc = acc_ref[:, head * BLOCK : (head + 1) * BLOCK]
+            acc = acc_ref[groups % 2, :, head * BLOCK : (head + 1) * BLOCK]
             out = acc[:HEAD_DIM] / acc[HEAD_DIM : HEAD_DIM + 1]
             o_ref[query_rows, head_cols(head)] = out.T.astype(jnp.bfloat16)
 
@@ -281,7 +326,7 @@
         scratch_shapes=[
             pltpu.VMEM((HEAD_DIM, per_kv * BLOCK), jnp.bfloat16),
             pltpu.VMEM((8, per_kv * BLOCK), jnp.float32),
-            pltpu.VMEM((HEAD_DIM + 16, per_kv * BLOCK), jnp.float32),
+            pltpu.VMEM((2, HEAD_DIM + 16, per_kv * BLOCK), jnp.float32),
         ],
         compiler_params=pltpu.CompilerParams(vmem_limit_bytes=30 * 1024 * 1024),
     )(entries, counts, queries, table)

time: 113 us -> 109 us (0.965)
  the two profiles are of different devices: /device:TPU:30 before, /device:TPU:4 now
where the time goes in v3:
time: 109 us
  Pallas kernels  104 us (95%)
  local copies, waits for them, and re-layouts  4.92 us (5%)
    pallas_call x1, Pallas kernels, gather(): pl.pallas_call(functools.partial(gather_kernel, shards, heads), out_shape...  70.7 us
    pallas_call x1, Pallas kernels, give_back(): pl.pallas_call(functools.partial(return_kernel, heads), out_shape=jax.Sha...  19.5 us
    pallas_call x1, Pallas kernels, attend(): pl.pallas_call(attend_kernel, out_shape=jax.ShapeDtypeStruct(queries.shap...  13.5 us
    unnamed x9, local copies, waits for them, and re-layouts  3.96 us

profile of v3, /device:TPU:4, one launch (start us, length us, event | category | flops | bytes accessed | tf_op | source)
XLA Modules:
  0.0 108.6 jit_solution(2808419620086576265)
XLA Ops:
  0.0 0.0 copy-start
  0.0 0.8 dynamic-slice_bitcast_fusion.count_ref
  0.8 0.2 copy-done
  1.0 0.1 constant_dynamic-slice_fusion
  1.0 0.1 copy.6
  1.1 0.0 copy-start.1
  1.1 1.1 %copy-done.1 = bf16[48,8192]{1,0:T(8,128)(2,1)S(1)} copy-done((bf16[48,8192]{1,0:T(8,128)(2,1)S(1)}, bf16[48,8192]{1,0:T(8,128)(2,1)}, u32[]{:S(2)}) %copy-start.1) | copy-done | bytes 786456
  2.3 0.0 copy-start.2
  2.3 0.9 copy-done.2
  3.2 0.0 copy-start.3
  3.2 0.9 copy-done.3
  4.0 70.7 %shard_map.55 = (bf16[384,1024]{1,0:T(8,128)(2,1)S(1)}, bf16[64,2,384,128]{3,2,1,0:T(8,128)(2,1)S(1)}) custom-call(bf16[48,8192]{1,0:T(8,128)(2,1)S(1)} %copy-done.1, bf16[48,1024]{1,0:T(8,128)(2,1)S(1)} %copy-done.2, bf16[48,1024]{1,0:T(8,128)(2,1)S(1)} %copy-done.3), custom_call_target="tpu_custom_call" | custom-call | tf_op jit(solution)/shard_map/pallas_call | solution.py:194
  74.8 13.5 %shard_map.56.o_ref = bf16[384,1024]{1,0:T(8,128)(2,1)S(1)} custom-call(s32[3,32]{1,0:T(4,128)S(1)} %bitcast.3, s32[3]{0:T(128)S(1)} %dynamic-slice_bitcast_fusion.count_ref, bf16[384,1024]{1,0:T(8,128)(2,1)S(1)} %get-tuple-element.7.q_ref, bf16[64,2,384,128]{3,2,1,0:T(8,128)(2,1)S(1)} %get-tuple-element.8.tab_ref), custom_call_target="tpu_custom_call" | custom-call | tf_op jit(solution)/shard_map/pallas_call | solution.py:321
  88.2 19.5 %shard_map.57 = bf16[48,8192]{1,0:T(8,128)(2,1)S(1)} custom-call(bf16[384,1024]{1,0:T(8,128)(2,1)S(1)} %shard_map.56.o_ref), custom_call_target="tpu_custom_call" | custom-call | tf_op jit(solution)/shard_map/pallas_call | solution.py:370
  107.8 0.9 copy.8
Async XLA Ops:
  0.0 1.0 copy-start
  1.1 1.1 %copy-start.1 = (bf16[48,8192]{1,0:T(8,128)(2,1)S(1)}, bf16[48,8192]{1,0:T(8,128)(2,1)}, u32[]{:S(2)}) copy-start(bf16[48,8192]{1,0:T(8,128)(2,1)} %q_ref.1) | copy-start | bytes 2359300
  2.3 0.9 copy-start.2
  3.2 0.9 copy-start.3

commit v4 on v3

--- a/solution.py
+++ b/solution.py
@@ -12,7 +12,7 @@
 KV_HEADS = 8
 HEAD_DIM = 128
 BLOCK = 128
-GROUP = 8
+GROUP = 16
 CHUNK = 1024
 LARGEST = 2.0**40
 EARLY_PART = (10, 24)
@@ -390,6 +390,9 @@
     width = block_list.shape[2]
     entries = lax.dynamic_slice(block_list, (h, s * blocks, 0), (1, blocks, width))[0]
     counts = lax.dynamic_slice(block_count, (h, s * blocks), (1, blocks))[0]
+    queries, keys, values = (
+        pltpu.with_memory_space_constraint(array, pltpu.HBM) for array in (queries, keys, values)
+    )
     query_local, table = gather(queries, keys, values, shards, heads)
     attended = attend(entries, counts, query_local, table)
     return give_back(attended, heads)

time: 109 us -> 107 us (0.982)
  local copies, waits for them, and re-layouts: 4.92 us -> 2 us
    unnamed x9 -> x3, local copies, waits for them, and re-layouts: 3.96 us -> 1.03 us
    pallas_call x1, Pallas kernels: 13.5 us -> 16.1 us  [attend(): pl.pallas_call(attend_kernel, out_shape=jax.ShapeDtypeStruct(queries.shap...]
    pallas_call x1, Pallas kernels: 19.5 us -> 17.7 us  [give_back(): pl.pallas_call(functools.partial(return_kernel, heads), out_shape=jax.Sha...]
where the time goes in v4:
time: 107 us
  Pallas kernels  105 us (98%)
  local copies, waits for them, and re-layouts  2 us (2%)
    pallas_call x1, Pallas kernels, gather(): pl.pallas_call(functools.partial(gather_kernel, shards, heads), out_shape...  70.9 us
    pallas_call x1, Pallas kernels, give_back(): pl.pallas_call(functools.partial(return_kernel, heads), out_shape=jax.Sha...  17.7 us
    pallas_call x1, Pallas kernels, attend(): pl.pallas_call(attend_kernel, out_shape=jax.ShapeDtypeStruct(queries.shap...  16.1 us

profile of v4, /device:TPU:4, one launch (start us, length us, event | category | flops | bytes accessed | tf_op | source)
XLA Modules:
  0.0 106.8 jit_solution(16550572252331363523)
XLA Ops:
  0.0 0.0 copy-start
  0.0 0.8 dynamic-slice_bitcast_fusion.count_ref
  0.8 0.2 copy-done
  1.0 0.1 constant_dynamic-slice_fusion
  1.0 0.1 copy.6
  1.1 70.9 %shard_map.55 = (bf16[384,1024]{1,0:T(8,128)(2,1)S(1)}, bf16[64,2,384,128]{3,2,1,0:T(8,128)(2,1)S(1)}) custom-call(bf16[48,8192]{1,0:T(8,128)(2,1)} %q_ref.1, bf16[48,1024]{1,0:T(8,128)(2,1)} %k_ref.1, bf16[48,1024]{1,0:T(8,128)(2,1)} %v_ref.1), custom_call_target="tpu_custom_call" | custom-call | tf_op jit(solution)/shard_map/pallas_call | solution.py:194
  72.0 16.1 %shard_map.56.o_ref = bf16[384,1024]{1,0:T(8,128)(2,1)S(1)} custom-call(s32[3,32]{1,0:T(4,128)S(1)} %bitcast.3, s32[3]{0:T(128)S(1)} %dynamic-slice_bitcast_fusion.count_ref, bf16[384,1024]{1,0:T(8,128)(2,1)S(1)} %get-tuple-element.7.q_ref, bf16[64,2,384,128]{3,2,1,0:T(8,128)(2,1)S(1)} %get-tuple-element.8.tab_ref), custom_call_target="tpu_custom_call" | custom-call | tf_op jit(solution)/shard_map/pallas_call | solution.py:321
  88.2 17.7 %shard_map.57 = bf16[48,8192]{1,0:T(8,128)(2,1)S(1)} custom-call(bf16[384,1024]{1,0:T(8,128)(2,1)S(1)} %shard_map.56.o_ref), custom_call_target="tpu_custom_call" | custom-call | tf_op jit(solution)/shard_map/pallas_call | solution.py:370
  105.9 0.9 copy.8
Async XLA Ops:
  0.0 1.0 copy-start

commit v5 on v4

--- a/solution.py
+++ b/solution.py
@@ -20,7 +20,13 @@
 CORES = 2
 HALVES = 2
 MESH = pl.DeviceIdType.MESH
+STEPS = ((1, 2), (1, 1), (1, 3), (1, 0), (0, 2), (0, 1), (0, 3))
 OWN, RING, EARLY, CROSS, MATE, MATE_EARLY, MATE_CROSS = range(7)
+
+
+def peers_of(h, heads):
+    half = heads // 2
+    return [(d + 1, (h // half + x) % 2 * half + (h % half + y) % half) for d, (x, y) in enumerate(STEPS)]
 
 
 def gather_kernel(
@@ -48,8 +54,8 @@
     here = pl.ds(pl.multiple_of(h * rows, 16), rows)
 
     barrier = pltpu.get_barrier_semaphore()
-    for d in range(1, heads):
-        pl.semaphore_signal(barrier, inc=1, device_id=(s, (h + d) % heads), device_id_type=MESH)
+    for _, peer in peers_of(h, heads):
+        pl.semaphore_signal(barrier, inc=1, device_id=(s, peer), device_id_type=MESH)
     for other in (up, down, mate, across):
         pl.semaphore_signal(barrier, inc=1, device_id=(other, h), device_id_type=MESH)
     pl.semaphore_wait(barrier, heads + 3)
@@ -60,8 +66,7 @@
         )
 
     kv_copies, q_copies = [], []
-    for d in range(1, heads):
-        peer = (h + d) % heads
+    for d, peer in peers_of(h, heads):
         cols = pl.ds(pl.multiple_of(peer * HEAD_DIM, HEAD_DIM), HEAD_DIM)
         for i, ref in enumerate((k_ref, v_ref)):
             kv_copies.append(
@@ -101,9 +106,18 @@
             return remote(ref, ref, send.at[kind, way, slot], recv.at[kind, way, slot], (to, h))
 
         def needed(kind, way, hops):
-            if kind != MATE or hops == 0:
+            if hops == 0:
                 return None
-            return z >= hops if way == 0 else z + hops >= depth
+            if kind == MATE:
+                return z >= hops if way == 0 else z + hops >= depth
+            if kind == RING and mine == 1:
+                return z >= hops if way == 0 else (z + hops) % depth < far
+            return None
+
+        def onward(way, hops):
+            if mine == 0:
+                return None
+            return (z >= hops) & (z + 1 < depth) if way == 0 else (z + hops) % depth < far
 
         def guarded(when, act):
             if when is None:
@@ -113,7 +127,7 @@
 
         def go(kind, way, hops):
             copy = copy_of(kind, way, hops + 1 if kind in (RING, EARLY) else hops, hops)
-            when = needed(kind, way, hops)
+            when = onward(way, hops) if kind == RING else needed(kind, way, hops)
             guarded(when, copy.start)
             sent.append((when, copy))
 
@@ -338,13 +352,12 @@
     s = lax.axis_index("seq")
     h = lax.axis_index("head")
     barrier = pltpu.get_barrier_semaphore()
-    for d in range(1, heads):
-        pl.semaphore_signal(barrier, inc=1, device_id=(s, (h + d) % heads), device_id_type=MESH)
+    for _, peer in peers_of(h, heads):
+        pl.semaphore_signal(barrier, inc=1, device_id=(s, peer), device_id_type=MESH)
     pl.semaphore_wait(barrier, heads - 1)
     mine = pl.ds(pl.multiple_of(h * cols, HEAD_DIM), cols)
     copies = []
-    for d in range(1, heads):
-        peer = (h + d) % heads
+    for d, peer in peers_of(h, heads):
         copies.append(
             pltpu.make_async_remote_copy(
                 src_ref=o_ref.at[pl.ds(pl.multiple_of(peer * rows, 16), rows)],

time: 107 us -> 108 us (level); the launches traced: 107 us -> 106 us
  no operation moved by 1% of the time
where the time goes in v5:
time: 108 us; the launch traced here: 106 us
  Pallas kernels  104 us (96%)
  local copies, waits for them, and re-layouts  2 us (2%)
    pallas_call x1, Pallas kernels, gather(): pl.pallas_call(functools.partial(gather_kernel, shards, heads), out_shape...  70.8 us
    pallas_call x1, Pallas kernels, give_back(): pl.pallas_call(functools.partial(return_kernel, heads), out_shape=jax.Sha...  16.9 us
    pallas_call x1, Pallas kernels, attend(): pl.pallas_call(attend_kernel, out_shape=jax.ShapeDtypeStruct(queries.shap...  16.1 us

profile of v5, /device:TPU:4, one launch (start us, length us, event | category | flops | bytes accessed | tf_op | source)
XLA Modules:
  0.0 105.9 jit_solution(2616747923385472793)
XLA Ops:
  0.0 0.0 copy-start
  0.0 0.8 dynamic-slice_bitcast_fusion.count_ref
  0.8 0.2 copy-done
  1.0 0.1 constant_dynamic-slice_fusion
  1.0 0.1 copy.6
  1.1 70.8 %shard_map.55 = (bf16[384,1024]{1,0:T(8,128)(2,1)S(1)}, bf16[64,2,384,128]{3,2,1,0:T(8,128)(2,1)S(1)}) custom-call(bf16[48,8192]{1,0:T(8,128)(2,1)} %q_ref.1, bf16[48,1024]{1,0:T(8,128)(2,1)} %k_ref.1, bf16[48,1024]{1,0:T(8,128)(2,1)} %v_ref.1), custom_call_target="tpu_custom_call" | custom-call | tf_op jit(solution)/shard_map/pallas_call | solution.py:208
  72.0 16.1 %shard_map.56.o_ref = bf16[384,1024]{1,0:T(8,128)(2,1)S(1)} custom-call(s32[3,32]{1,0:T(4,128)S(1)} %bitcast.3, s32[3]{0:T(128)S(1)} %dynamic-slice_bitcast_fusion.count_ref, bf16[384,1024]{1,0:T(8,128)(2,1)S(1)} %get-tuple-element.7.q_ref, bf16[64,2,384,128]{3,2,1,0:T(8,128)(2,1)S(1)} %get-tuple-element.8.tab_ref), custom_call_target="tpu_custom_call" | custom-call | tf_op jit(solution)/shard_map/pallas_call | solution.py:335
  88.1 16.9 %shard_map.57 = bf16[48,8192]{1,0:T(8,128)(2,1)S(1)} custom-call(bf16[384,1024]{1,0:T(8,128)(2,1)S(1)} %shard_map.56.o_ref), custom_call_target="tpu_custom_call" | custom-call | tf_op jit(solution)/shard_map/pallas_call | solution.py:383
  105.0 0.9 copy.8
Async XLA Ops:
  0.0 1.0 copy-start
